TPU v7x, 32 devices: a whole 2x2x4 slice. The times are simulated.
32 devices in a mesh: dp: 8 (over z, y), mp: 4 (over x, core).
Axes of the slice: x: 2, y: 2, z: 4, core: 2. Of those that a mesh axis runs over, the one named last changes fastest.
Arguments:
- activations: bfloat16 [4, 4096, 5120], P(None, 'dp'), may hold values from -60 to 60
- task_weights: bfloat16 [4, 5120, 512], P(None, 'dp', 'mp'), may hold values from -6 to 6
Outputs:
- merged: float32 [5120, 512], P('dp', 'mp')
All inputs are finite; a program needn't handle non-finite values.
Results may differ from a plain program's by a relative error of at most 0.0015.
Values may be sent and summed in bfloat16 or wider, within the bound.
A program may use at most 128 MiB of HBM per device.

v0:
```python
import jax
import jax.numpy as jnp
from jax import lax
from jax.sharding import PartitionSpec as P

ALPHA = 0.9


def dot(left, right, dims):
    return lax.dot_general(left, right, (dims, ((), ())), preferred_element_type=jnp.float32)


def rounded(array):
    return lax.reduce_precision(array, 8, 7)


def split_pair(array):
    coarse = rounded(array)
    high = coarse.astype(jnp.bfloat16)
    low = (array - coarse).astype(jnp.bfloat16)
    return jnp.concatenate([high, low], axis=1)


def shards(activations, task_weights):
    tasks, tokens, width = activations.shape
    cols = task_weights.shape[2]
    total = tasks * tokens * lax.axis_size("dp")
    bf16, f32 = (jnp.bfloat16, jnp.float32)
    flat = activations.reshape(tasks * tokens, width)
    weights = lax.all_gather(task_weights, "dp", axis=1, tiled=True)
    squares = jnp.sum(jnp.square(activations.astype(f32)), axis=1)
    squares_all = jnp.sum(squares, axis=0)[:, None]
    mean = jnp.mean(weights.astype(f32), axis=0)
    mean_pair = split_pair(mean)
    gaps = []
    for task in range(tasks):
        wide = dot(
            activations[task], jnp.concatenate([weights[task], mean_pair], axis=1), ((1,), (0,))
        )
        outputs = rounded(wide[:, :cols])
        gaps.append(outputs - (wide[:, cols : 2 * cols] + wide[:, 2 * cols :]))
    gap = split_pair(jnp.concatenate(gaps, axis=0))
    diag = sum((squares[t][:, None] * (weights[t].astype(f32) - mean) for t in range(tasks)))
    inner = dot(flat, gap, ((0,), (0,)))
    inner = inner[:, :cols] + inner[:, cols:]
    residual = lax.psum_scatter(
        (ALPHA * inner + (1.0 - ALPHA) * diag) / total, "dp", scatter_dimension=0, tiled=True
    )
    full_bf = lax.all_gather(residual.astype(bf16), "dp", axis=0, tiled=True)
    full = full_bf.astype(f32)
    projected = split_pair(dot(flat, full_bf, ((1,), (0,))))
    inner = dot(flat, projected, ((0,), (0,)))
    inner = inner[:, :cols] + inner[:, cols:]
    image = lax.psum_scatter(
        (ALPHA * inner + (1.0 - ALPHA) * squares_all * full) / total,
        "dp",
        scatter_dimension=0,
        tiled=True,
    )
    image_full = lax.all_gather(image.astype(bf16), "dp", axis=0, tiled=True).astype(f32)
    norm0 = jnp.sum(full * full, axis=0)
    alpha0 = norm0 / jnp.sum(full * image_full, axis=0)
    next_full = full - alpha0 * image_full
    norm1 = jnp.sum(next_full * next_full, axis=0)
    beta = norm1 / norm0
    direction = next_full + beta * full
    direction_bf = direction.astype(bf16)
    direction = direction_bf.astype(f32)
    projected = dot(flat, direction_bf, ((1,), (0,)))
    energy = lax.psum(
        (
            ALPHA * jnp.sum(projected * projected, axis=0)
            + (1.0 - ALPHA) * jnp.sum(squares_all * direction * direction, axis=0)
        )
        / total,
        "dp",
    )
    alpha1 = norm1 / energy
    own_mean = jnp.mean(task_weights.astype(f32), axis=0)
    return own_mean + alpha0 * residual + alpha1 * (residual - alpha0 * image + beta * residual)


def solution(mesh):
    return jax.shard_map(
        shards,
        mesh=mesh,
        in_specs=(P(None, "dp", None), P(None, "dp", "mp")),
        out_specs=P("dp", "mp"),
        check_vma=False,
    )
```

profile of v0, /device:TPU:0, one launch (start us, length us, event | category | flops | bytes accessed | tf_op | source)
XLA Modules:
  0.0 432.0 jit_solution(4052554290245626200)
XLA Ops:
  6.5 2.2 copy.6
  8.8 9.5 %fusion = (f32[5120]{0:T(1024)S(1)}, f32[4,5120]{1,0:T(4,128)S(1)}) fusion(bf16[4,512,5120]{2,1,0:T(8,128)(2,1)} %param.2), kind=kLoop, calls=%fused_computation.1 | loop fusion | flops 41917440 | bytes 21073920 | tf_op jit(solution)/shard_map/reduce_sum | solution.py:32
  18.3 0.7 fusion.62
  18.9 79.0 %all-gather.4.cloned.1.call-done = bf16[4,5120,128]{1,2,0:T(8,128)(2,1)} async-done(((bf16[4,640,128]{1,2,0:T(8,128)(2,1)}), bf16[4,5120,128]{1,2,0:T(8,128)(2,1)}) %all-gather.4.cloned.1.call-update) | async-done | bytes 5242896 | tf_op jit(solution)/shard_map/all_gather | solution.py:30
  97.9 3.8 convert_reduce_fusion
  101.8 0.5 reduce-precision_convert_fusion
  102.3 2.1 slice_bitcast_fusion.3
  104.4 6.9 %fusion.30 = f32[512,384]{0,1:T(8,128)} fusion(bf16[4,512,5120]{2,1,0:T(8,128)(2,1)} %param.2, bf16[5120,128]{0,1:T(8,128)(2,1)S(1)} %get-tuple-element.16, bf16[5120,128]{0,1:T(8,128)(2,1)S(1)} %get-tuple-element.15, bf16[5120,128]{0,1:T(8,128)(2,1)} %get-tuple-element.11), kind=kOutput, calls=%fused_computation.65 | convolution fusion | flops 2025062400 | bytes 9961472 | tf_op jit(solution)/shard_map/dot_general | solution.py:10
  111.3 1.3 slice-done.4
  112.6 4.7 %fusion.33 = f32[512,384]{0,1:T(8,128)} fusion(bf16[4,512,5120]{2,1,0:T(8,128)(2,1)S(1)} %bitcast.65, bf16[5120,128]{0,1:T(8,128)(2,1)S(1)} %get-tuple-element.16, bf16[5120,128]{0,1:T(8,128)(2,1)S(1)} %get-tuple-element.15, bf16[5120,128]{0,1:T(8,128)(2,1)} %get-tuple-element.14), kind=kOutput, calls=%fused_computation.66 | convolution fusion | flops 2025062400 | bytes 9961472 | tf_op jit(solution)/shard_map/dot_general | solution.py:10
  117.2 3.7 fusion.36
  120.9 3.3 fusion.39
  124.2 1.6 fusion.53
  126.0 0.2 reduce-precision_convert_fusion.2
  126.2 7.6 %convolution_bitcast_fusion.1 = f32[5120,256]{0,1:T(8,128)} fusion(bf16[2048,5120]{1,0:T(8,128)(2,1)S(1)} %bitcast.66, bf16[2048,128]{0,1:T(8,128)(2,1)S(1)} %get-tuple-element.20, bf16[2048,128]{0,1:T(8,128)(2,1)S(1)} %get-tuple-element.19), kind=kOutput, calls=%fused_computation.5 | convolution fusion | flops 5370806272 | bytes 27262976 | tf_op jit(solution)/shard_map/dot_general | solution.py:10
  133.8 6.0 %fusion.29 = f32[5120,128]{0,1:T(8,128)} fusion(f32[5120,256]{0,1:T(8,128)} %convolution_bitcast_fusion.1, f32[5120,128]{0,1:T(8,128)S(1)} %convert_reduce_fusion, f32[5120]{0:T(1024)S(1)} %bitcast.68, f32[5120]{0:T(1024)S(1)} %bitcast.69, f32[5120]{0:T(1024)S(1)} %bitcast.70, f32[5120]{0:T(1024)S(1)} %bitcast.67, ...), kind=kLoop, calls=%fused_computation.52 | loop fusion | flops 13762560 | bytes 15810560 | tf_op jit(solution)/shard_map/div | solution.py:47
  139.9 69.6 %reduce-scatter.3.cloned.1.call-done = f32[640,128]{0,1:T(8,128)} async-done(((f32[5120,128]{0,1:T(8,128)}), f32[640,128]{0,1:T(8,128)}) %reduce-scatter.3.cloned.1.call-update) | async-done | bytes 327696 | tf_op jit(solution)/shard_map/reduce_scatter | solution.py:46
  209.4 1.7 convert_element_type.68
  211.2 42.2 %all-gather.6.cloned.1.call-done = bf16[5120,128]{0,1:T(8,128)(2,1)} async-done(((bf16[640,128]{0,1:T(8,128)(2,1)}), bf16[5120,128]{0,1:T(8,128)(2,1)}) %all-gather.6.cloned.1.call-update) | async-done | bytes 1310736 | tf_op jit(solution)/shard_map/all_gather | solution.py:49
  253.4 11.6 %reduce-precision_convert_fusion.1 = (bf16[2048,128]{0,1:T(8,128)(2,1)S(1)}, bf16[2048,128]{0,1:T(8,128)(2,1)S(1)}) fusion(bf16[5120,128]{0,1:T(8,128)(2,1)} %all-gather.6.cloned.1.call-done, bf16[2048,5120]{1,0:T(8,128)(2,1)} %bitcast.61), kind=kOutput, calls=%fused_computation.57 | convolution fusion | flops 2685403136 | bytes 23330816 | tf_op jit(solution)/shard_map/dot_general | solution.py:10
  265.0 10.0 %convolution_bitcast_fusion = f32[5120,256]{0,1:T(8,128)S(1)} fusion(bf16[2048,5120]{1,0:T(8,128)(2,1)} %bitcast.62, bf16[2048,128]{0,1:T(8,128)(2,1)S(1)} %get-tuple-element.18, bf16[2048,128]{0,1:T(8,128)(2,1)S(1)} %get-tuple-element.17), kind=kOutput, calls=%fused_computation.4 | convolution fusion | flops 5370806272 | bytes 27262976 | tf_op jit(solution)/shard_map/dot_general | solution.py:10
  275.0 2.0 fusion.22
  277.1 69.6 %reduce-scatter.5.cloned.1.call-done = f32[640,128]{0,1:T(8,128)} async-done(((f32[5120,128]{0,1:T(8,128)}), f32[640,128]{0,1:T(8,128)}) %reduce-scatter.5.cloned.1.call-update) | async-done | bytes 327696 | tf_op jit(solution)/shard_map/reduce_scatter | solution.py:54
  346.6 1.7 convert_element_type.72
  348.6 41.8 %all-gather.8.cloned.1.call-done = bf16[5120,128]{0,1:T(8,128)(2,1)} async-done(((bf16[640,128]{0,1:T(8,128)(2,1)}), bf16[5120,128]{0,1:T(8,128)(2,1)}) %all-gather.8.cloned.1.call-update) | async-done | bytes 1310736 | tf_op jit(solution)/shard_map/all_gather | solution.py:60
  390.4 2.0 fusion.23
  392.5 0.7 multiply_reduce_fusion
  393.1 1.1 fusion.19
  394.3 11.1 %fusion.42 = f32[128]{0:T(128)S(1)} fusion(bf16[5120,128]{0,1:T(8,128)(2,1)S(1)} %get-tuple-element.10, bf16[2048,5120]{1,0:T(8,128)(2,1)} %bitcast.63), kind=kOutput, calls=%fused_computation.69 | convolution fusion | flops 2684878848 | bytes 22282752 | tf_op jit(solution)/shard_map/dot_general | solution.py:10
  405.4 19.0 %psum.7 = f32[128]{0:T(128)S(1)} all-reduce(f32[128]{0:T(128)S(1)} %add_multiply_fusion), channel_id=1, replica_groups=mesh['dp'=8,'mp'=4] {'dp'}, use_global_device_ids=true, to_apply=%region_11.0 | all-reduce | flops 128 | bytes 1024 | tf_op jit(solution)/shard_map/psum | solution.py:70
  424.4 0.2 multiply_add_fusion
  424.6 0.9 copy.7
  (44 shorter events, 0.8 us)
Async XLA Ops:
  6.5 91.4 %all-gather.4.cloned.1.call-start = ((), (), s32[]{:S(2)}) async-start(), calls=%async_computation.2 | async-start | bytes 5898240 | tf_op jit(solution)/shard_map/all_gather | solution.py:30
  8.8 200.7 %reduce-scatter.3.cloned.1.call-start = ((), (), s32[]{:S(2)}) async-start(), calls=%async_computation.3 | async-start | bytes 2949120 | tf_op jit(solution)/shard_map/reduce_scatter | solution.py:46
  97.9 4.3 copy-start
  101.7 9.5 %slice-start = ((s8[20971520]{0:T(1024)(128)(4,1)}), s8[4194304]{0:T(1024)(128)(4,1)S(1)}, s32[]{:S(2)}) async-start(s8[20971520]{0:T(1024)(128)(4,1)} %bitcast.64), calls=%async_computation.7 | async-start | bytes 8388608
  102.2 9.0 %slice-start.1 = ((s8[20971520]{0:T(1024)(128)(4,1)}), s8[4194304]{0:T(1024)(128)(4,1)S(1)}, s32[]{:S(2)}) async-start(s8[20971520]{0:T(1024)(128)(4,1)} %bitcast.64), calls=%async_computation.8 | async-start | bytes 8388608
  102.3 9.0 %slice-start.2 = ((s8[20971520]{0:T(1024)(128)(4,1)}), s8[4194304]{0:T(1024)(128)(4,1)S(1)}, s32[]{:S(2)}) async-start(s8[20971520]{0:T(1024)(128)(4,1)} %bitcast.64), calls=%async_computation.9 | async-start | bytes 8388608
  104.4 6.9 %slice-start.3 = ((s8[20971520]{0:T(1024)(128)(4,1)}), s8[4194304]{0:T(1024)(128)(4,1)S(1)}, s32[]{:S(2)}) async-start(s8[20971520]{0:T(1024)(128)(4,1)} %bitcast.64), calls=%async_computation.10 | async-start | bytes 8388608
  104.4 8.2 %slice-start.4 = ((s8[20971520]{0:T(1024)(128)(4,1)}), s8[4194304]{0:T(1024)(128)(4,1)S(1)}, s32[]{:S(2)}) async-start(s8[20971520]{0:T(1024)(128)(4,1)} %bitcast.64), calls=%async_computation.11 | async-start | bytes 8388608
  124.2 1.6 copy-start.6
  126.1 7.6 %copy-start.7 = (f32[1,5120]{1,0:T(1,128)S(1)}, f32[1,5120]{1,0:T(1,128)}, u32[]{:S(2)}) copy-start(f32[1,5120]{1,0:T(1,128)} %get-tuple-element.24) | copy-start | bytes 61444
  139.8 113.5 %all-gather.6.cloned.1.call-start = ((), (), s32[]{:S(2)}) async-start(), calls=%async_computation.4 | async-start | bytes 1474560 | tf_op jit(solution)/shard_map/all_gather | solution.py:49
  211.1 135.5 %reduce-scatter.5.cloned.1.call-start = ((), (), s32[]{:S(2)}) async-start(), calls=%async_computation.5 | async-start | bytes 2949120 | tf_op jit(solution)/shard_map/reduce_scatter | solution.py:54
  265.0 10.0 %copy-start.1 = (bf16[5120,128]{0,1:T(8,128)(2,1)S(1)}, bf16[5120,128]{0,1:T(8,128)(2,1)}, u32[]{:S(2)}) copy-start(bf16[5120,128]{0,1:T(8,128)(2,1)} %all-gather.6.cloned.1.call-done) | copy-start | bytes 3932164
  277.0 71.3 %copy-start.3 = (bf16[4,640,128]{2,1,0:T(8,128)(2,1)S(1)}, bf16[4,640,128]{2,1,0:T(8,128)(2,1)}, u32[]{:S(2)}) copy-start(bf16[4,640,128]{2,1,0:T(8,128)(2,1)} %param.3) | copy-start | bytes 1966084
  277.0 113.4 %all-gather.8.cloned.1.call-start = ((), (), s32[]{:S(2)}) async-start(), calls=%async_computation.6 | async-start | bytes 1474560 | tf_op jit(solution)/shard_map/all_gather | solution.py:60
  390.4 2.0 copy-start.2
  394.3 30.2 %copy-start.4 = (f32[640,128]{0,1:T(8,128)S(1)}, f32[640,128]{0,1:T(8,128)}, u32[]{:S(2)}) copy-start(f32[640,128]{0,1:T(8,128)} %reduce-scatter.3.cloned.1.call-done) | copy-start | bytes 983044
  394.3 30.1 %copy-start.5 = (f32[640,128]{0,1:T(8,128)S(1)}, f32[640,128]{0,1:T(8,128)}, u32[]{:S(2)}) copy-start(f32[640,128]{0,1:T(8,128)} %reduce-scatter.5.cloned.1.call-done) | copy-start | bytes 983044
Sparse Core Ops, SparseCore 0:
  9.5 88.3 all-gather.3
  139.9 69.4 reduce-scatter.2
  211.7 41.6 all-gather.5
  277.2 69.4 reduce-scatter.4
  348.7 41.6 all-gather.7
where the time goes:
time: 432 us
  waiting for transfers between devices  302 us (70%)
  matrix products  58.9 us (14%)
  other arithmetic  31.1 us (7%)
  blocking collectives  19 us (4%)
  between operations  13.3 us (3%)
  local copies, waits for them, and re-layouts  7.36 us (2%)
    all_gather x1, waiting for transfers between devices, shards(): weights = lax.all_gather(task_weights, 'dp', axis=1, tiled=True)  79 us
    reduce_scatter x1, waiting for transfers between devices, shards(): lax.psum_scatter((ALPHA * inner + (1.0 - ALPHA) * diag) / total, 'dp', sc...  69.6 us
    reduce_scatter x1, waiting for transfers between devices, shards(): lax.psum_scatter((ALPHA * inner + (1.0 - ALPHA) * squares_all * full) / t...  69.6 us
    dot_general x8, matrix products, dot(): lax.dot_general(left, right, (dims, ((), ())), preferred_element_type=jnp...  58.9 us
    all_gather x1, waiting for transfers between devices, shards(): full_bf = lax.all_gather(residual.astype(bf16), 'dp', axis=0, tiled=True)  42.2 us
    all_gather x1, waiting for transfers between devices, shards(): lax.all_gather(image.astype(bf16), 'dp', axis=0, tiled=True).astype(f32)  41.8 us
    psum x1, blocking collectives, shards(): lax.psum((ALPHA * jnp.sum(projected * projected, axis=0) + (1.0 - ALPHA)...  19 us
    reduce_sum x1, other arithmetic, shards(): squares_all = jnp.sum(squares, axis=0)[:, None]  9.47 us
  transfers between devices with their start and end apart: 5, of which 5 were waited for; matrix products, arithmetic and copies ran while one was open for 2% of the time, Pallas kernels for 0%

commit v1 on v0

--- a/solution.py
+++ b/solution.py
@@ -2,6 +2,7 @@
 import jax.numpy as jnp
 from jax import lax
 from jax.sharding import PartitionSpec as P
+from jax.lax import axis_index, axis_size, ppermute
 
 ALPHA = 0.9
 
@@ -27,7 +28,29 @@
     total = tasks * tokens * lax.axis_size("dp")
     bf16, f32 = (jnp.bfloat16, jnp.float32)
     flat = activations.reshape(tasks * tokens, width)
-    weights = lax.all_gather(task_weights, "dp", axis=1, tiled=True)
+    z_new, earlier, plain = (axis_size("dp"), axis_index("dp"), task_weights.shape[1])
+    weights = lax.dynamic_update_slice_in_dim(
+        jnp.zeros(
+            [d * z_new if j0 == 1 else d for j0, d in enumerate(task_weights.shape)],
+            task_weights.dtype,
+        ),
+        task_weights,
+        earlier * plain,
+        axis=1,
+    )
+    current_block = oldest = task_weights
+    for jj in range(1, z_new // 2 + 1):
+        current_block = ppermute(
+            current_block, "dp", [(j0, (j0 + 1) % z_new) for j0 in range(z_new)]
+        )
+        weights = lax.dynamic_update_slice_in_dim(
+            weights, current_block, (earlier - jj) % z_new * plain, axis=1
+        )
+        if 2 * jj < z_new:
+            oldest = ppermute(oldest, "dp", [(j0, (j0 - 1) % z_new) for j0 in range(z_new)])
+            weights = lax.dynamic_update_slice_in_dim(
+                weights, oldest, (earlier + jj) % z_new * plain, axis=1
+            )
     squares = jnp.sum(jnp.square(activations.astype(f32)), axis=1)
     squares_all = jnp.sum(squares, axis=0)[:, None]
     mean = jnp.mean(weights.astype(f32), axis=0)

time: 432 us -> 458 us (1.060)
  starting transfers between devices: 0.17 us -> 16.8 us
  local copies, waits for them, and re-layouts: 7.36 us -> 21.1 us
  waiting for transfers between devices: 302 us -> 295 us
    all_gather x1 -> x0, waiting for transfers between devices: 79 us -> none  [shards(): weights = lax.all_gather(task_weights, 'dp', axis=1, tiled=True)]
    ppermute x0 -> x7, waiting for transfers between devices: none -> 73 us  [the longest x4 48.6 us: shards(): ppermute(current_block, 'dp', [(j0, (j0 + 1) % z_new) for j0 in range(z_n...]
    ppermute x0 -> x7, starting transfers between devices: none -> 16.7 us  [the longest x4 10.5 us: shards(): ppermute(current_block, 'dp', [(j0, (j0 + 1) % z_new) for j0 in range(z_n...]
    dynamic_update_slice x0 -> x8, local copies, waits for them, and re-layouts: none -> 9.85 us  [the longest x3 5.05 us: shards(): lax.dynamic_update_slice_in_dim(weights, oldest, (earlier + jj) % z_new *...]
  transfers between devices with their start and end apart: 5 -> 11, of which waited for: 5 -> 9; matrix products, arithmetic and copies ran while one was open for 2% -> 5% of each run, Pallas kernels for 0% -> 0%
where the time goes in v1:
time: 458 us
  waiting for transfers between devices  295 us (64%)
  matrix products  60.9 us (13%)
  other arithmetic  31.1 us (7%)
  local copies, waits for them, and re-layouts  21.1 us (5%)
  blocking collectives  19 us (4%)
  starting transfers between devices  16.8 us (4%)
  between operations  13.4 us (3%)
    reduce_scatter x1, waiting for transfers between devices, shards(): lax.psum_scatter((ALPHA * inner + (1.0 - ALPHA) * squares_all * full) / t...  69.7 us
    reduce_scatter x1, waiting for transfers between devices, shards(): lax.psum_scatter((ALPHA * inner + (1.0 - ALPHA) * diag) / total, 'dp', sc...  68.5 us
    dot_general x8, matrix products, dot(): lax.dot_general(left, right, (dims, ((), ())), preferred_element_type=jnp...  60.9 us
    ppermute x4, waiting for transfers between devices, shards(): ppermute(current_block, 'dp', [(j0, (j0 + 1) % z_new) for j0 in range(z_n...  48.6 us
    all_gather x1, waiting for transfers between devices, shards(): full_bf = lax.all_gather(residual.astype(bf16), 'dp', axis=0, tiled=True)  42.2 us
    all_gather x1, waiting for transfers between devices, shards(): lax.all_gather(image.astype(bf16), 'dp', axis=0, tiled=True).astype(f32)  41.9 us
    ppermute x3, waiting for transfers between devices, shards(): ppermute(oldest, 'dp', [(j0, (j0 - 1) % z_new) for j0 in range(z_new)])  24.5 us
    psum x1, blocking collectives, shards(): lax.psum((ALPHA * jnp.sum(projected * projected, axis=0) + (1.0 - ALPHA)...  19 us
  transfers between devices with their start and end apart: 11, of which 9 were waited for; matrix products, arithmetic and copies ran while one was open for 5% of the time, Pallas kernels for 0%

profile of v1, /device:TPU:0, one launch (start us, length us, event | category | flops | bytes accessed | tf_op | source)
XLA Modules:
  0.0 457.6 jit_solution(15455807735661261472)
XLA Ops:
  7.9 3.0 collective-permute-start
  11.0 3.1 collective-permute-start.1
  14.1 24.9 %collective-permute-done = bf16[4,640,128]{1,2,0:T(8,128)(2,1)S(1)} collective-permute-done((bf16[4,640,128]{1,2,0:T(8,128)(2,1)S(1)}, bf16[4,640,128]{1,2,0:T(8,128)(2,1)S(1)}, u32[]{:S(2)}, u32[]{:S(2)}) %collective-permute-start) | collective-permute-done | bytes 655392 | tf_op jit(solution)/shard_map/ppermute | solution.py:43
  39.0 2.5 collective-permute-start.2
  41.5 9.5 %fusion = (f32[5120]{0:T(1024)S(1)}, f32[4,5120]{1,0:T(4,128)S(1)}) fusion(bf16[4,512,5120]{2,1,0:T(8,128)(2,1)} %param.2), kind=kLoop, calls=%fused_computation.1 | loop fusion | flops 41917440 | bytes 21073920 | tf_op jit(solution)/shard_map/reduce_sum | solution.py:55
  51.0 3.1 collective-permute-start.3
  54.1 14.6 %collective-permute-done.2 = bf16[4,640,128]{1,2,0:T(8,128)(2,1)S(1)} collective-permute-done((bf16[4,640,128]{1,2,0:T(8,128)(2,1)S(1)}, bf16[4,640,128]{1,2,0:T(8,128)(2,1)S(1)}, u32[]{:S(2)}, u32[]{:S(2)}) %collective-permute-start.2) | collective-permute-done | bytes 655392 | tf_op jit(solution)/shard_map/ppermute | solution.py:43
  68.7 2.5 collective-permute-start.4
  71.8 14.8 %collective-permute-done.3 = bf16[4,640,128]{1,2,0:T(8,128)(2,1)} collective-permute-done((bf16[4,640,128]{1,2,0:T(8,128)(2,1)S(1)}, bf16[4,640,128]{1,2,0:T(8,128)(2,1)}, u32[]{:S(2)}, u32[]{:S(2)}) %collective-permute-start.3) | collective-permute-done | bytes 655392 | tf_op jit(solution)/shard_map/ppermute | solution.py:50
  86.6 3.0 broadcast_in_dim.2
  90.5 9.0 %collective-permute-done.4 = bf16[4,640,128]{1,2,0:T(8,128)(2,1)S(1)} collective-permute-done((bf16[4,640,128]{1,2,0:T(8,128)(2,1)S(1)}, bf16[4,640,128]{1,2,0:T(8,128)(2,1)S(1)}, u32[]{:S(2)}, u32[]{:S(2)}) %collective-permute-start.4) | collective-permute-done | bytes 655392 | tf_op jit(solution)/shard_map/ppermute | solution.py:43
  99.6 2.5 collective-permute-start.6
  104.9 2.0 constant_dynamic-update-slice_fusion.3
  107.9 9.7 %collective-permute-done.5 = bf16[4,640,128]{1,2,0:T(8,128)(2,1)} collective-permute-done((bf16[4,640,128]{1,2,0:T(8,128)(2,1)}, bf16[4,640,128]{1,2,0:T(8,128)(2,1)}, u32[]{:S(2)}, u32[]{:S(2)}) %collective-permute-start.5) | collective-permute-done | bytes 655392 | tf_op jit(solution)/shard_map/ppermute | solution.py:50
  117.6 2.0 constant_dynamic-update-slice_fusion.1
  120.6 4.2 slice_bitcast_fusion.3
  124.8 3.8 convert_reduce_fusion
  130.6 7.0 %fusion.30 = f32[512,384]{0,1:T(8,128)} fusion(bf16[4,512,5120]{2,1,0:T(8,128)(2,1)} %param.2, bf16[5120,128]{0,1:T(8,128)(2,1)} %get-tuple-element.16, bf16[5120,128]{0,1:T(8,128)(2,1)} %get-tuple-element.15, bf16[5120,128]{0,1:T(8,128)(2,1)} %get-tuple-element.11), kind=kOutput, calls=%fused_computation.65 | convolution fusion | flops 2025062400 | bytes 9961472 | tf_op jit(solution)/shard_map/dot_general | solution.py:11
  137.6 4.8 %fusion.33 = f32[512,384]{0,1:T(8,128)} fusion(bf16[4,512,5120]{2,1,0:T(8,128)(2,1)S(1)} %bitcast.65, bf16[5120,128]{0,1:T(8,128)(2,1)} %get-tuple-element.16, bf16[5120,128]{0,1:T(8,128)(2,1)} %get-tuple-element.15, bf16[5120,128]{0,1:T(8,128)(2,1)S(1)} %get-tuple-element.14), kind=kOutput, calls=%fused_computation.66 | convolution fusion | flops 2025062400 | bytes 9961472 | tf_op jit(solution)/shard_map/dot_general | solution.py:11
  142.4 4.1 fusion.36
  146.6 4.6 %fusion.39 = f32[512,384]{0,1:T(8,128)} fusion(bf16[4,512,5120]{2,1,0:T(8,128)(2,1)S(1)} %bitcast.65, bf16[5120,128]{0,1:T(8,128)(2,1)} %get-tuple-element.16, bf16[5120,128]{0,1:T(8,128)(2,1)S(1)} %copy-done.3, bf16[5120,128]{0,1:T(8,128)(2,1)S(1)} %get-tuple-element.12), kind=kOutput, calls=%fused_computation.68 | convolution fusion | flops 2025062400 | bytes 9961472 | tf_op jit(solution)/shard_map/dot_general | solution.py:11
  152.7 7.6 %convolution_bitcast_fusion.1 = f32[5120,256]{0,1:T(8,128)} fusion(bf16[2048,5120]{1,0:T(8,128)(2,1)S(1)} %bitcast.66, bf16[2048,128]{0,1:T(8,128)(2,1)S(1)} %get-tuple-element.20, bf16[2048,128]{0,1:T(8,128)(2,1)S(1)} %get-tuple-element.19), kind=kOutput, calls=%fused_computation.5 | convolution fusion | flops 5370806272 | bytes 27262976 | tf_op jit(solution)/shard_map/dot_general | solution.py:11
  160.3 6.0 %fusion.29 = f32[5120,128]{0,1:T(8,128)} fusion(f32[5120,256]{0,1:T(8,128)} %convolution_bitcast_fusion.1, f32[5120,128]{0,1:T(8,128)S(1)} %convert_reduce_fusion, f32[5120]{0:T(1024)S(1)} %bitcast.68, f32[5120]{0:T(1024)S(1)} %bitcast.69, f32[5120]{0:T(1024)S(1)} %bitcast.70, f32[5120]{0:T(1024)S(1)} %bitcast.67, ...), kind=kLoop, calls=%fused_computation.52 | loop fusion | flops 13762560 | bytes 15810560 | tf_op jit(solution)/shard_map/div | solution.py:70
  166.4 68.5 %reduce-scatter.3.cloned.1.call-done = f32[640,128]{0,1:T(8,128)} async-done(((f32[5120,128]{0,1:T(8,128)}), f32[640,128]{0,1:T(8,128)}) %reduce-scatter.3.cloned.1.call-update) | async-done | bytes 327696 | tf_op jit(solution)/shard_map/reduce_scatter | solution.py:69
  236.6 42.2 %all-gather.3.cloned.1.call-done = bf16[5120,128]{0,1:T(8,128)(2,1)} async-done(((bf16[640,128]{0,1:T(8,128)(2,1)}), bf16[5120,128]{0,1:T(8,128)(2,1)}) %all-gather.3.cloned.1.call-update) | async-done | bytes 1310736 | tf_op jit(solution)/shard_map/all_gather | solution.py:72
  278.8 11.6 %reduce-precision_convert_fusion.1 = (bf16[2048,128]{0,1:T(8,128)(2,1)S(1)}, bf16[2048,128]{0,1:T(8,128)(2,1)S(1)}) fusion(bf16[5120,128]{0,1:T(8,128)(2,1)} %all-gather.3.cloned.1.call-done, bf16[2048,5120]{1,0:T(8,128)(2,1)} %bitcast.61), kind=kOutput, calls=%fused_computation.57 | convolution fusion | flops 2685403136 | bytes 23330816 | tf_op jit(solution)/shard_map/dot_general | solution.py:11
  290.4 10.0 %convolution_bitcast_fusion = f32[5120,256]{0,1:T(8,128)S(1)} fusion(bf16[2048,5120]{1,0:T(8,128)(2,1)} %bitcast.62, bf16[2048,128]{0,1:T(8,128)(2,1)S(1)} %get-tuple-element.18, bf16[2048,128]{0,1:T(8,128)(2,1)S(1)} %get-tuple-element.17), kind=kOutput, calls=%fused_computation.4 | convolution fusion | flops 5370806272 | bytes 27262976 | tf_op jit(solution)/shard_map/dot_general | solution.py:11
  300.4 2.0 fusion.22
  302.5 69.7 %reduce-scatter.5.cloned.1.call-done = f32[640,128]{0,1:T(8,128)} async-done(((f32[5120,128]{0,1:T(8,128)}), f32[640,128]{0,1:T(8,128)}) %reduce-scatter.5.cloned.1.call-update) | async-done | bytes 327696 | tf_op jit(solution)/shard_map/reduce_scatter | solution.py:77
  374.1 41.9 %all-gather.5.cloned.1.call-done = bf16[5120,128]{0,1:T(8,128)(2,1)} async-done(((bf16[640,128]{0,1:T(8,128)(2,1)}), bf16[5120,128]{0,1:T(8,128)(2,1)}) %all-gather.5.cloned.1.call-update) | async-done | bytes 1310736 | tf_op jit(solution)/shard_map/all_gather | solution.py:83
  419.8 11.1 %fusion.42 = f32[128]{0:T(128)S(1)} fusion(bf16[5120,128]{0,1:T(8,128)(2,1)S(1)} %get-tuple-element.10, bf16[2048,5120]{1,0:T(8,128)(2,1)} %bitcast.63), kind=kOutput, calls=%fused_computation.69 | convolution fusion | flops 2684878848 | bytes 22282752 | tf_op jit(solution)/shard_map/dot_general | solution.py:11
  431.0 19.0 %psum.7 = f32[128]{0:T(128)S(1)} all-reduce(f32[128]{0:T(128)S(1)} %add_multiply_fusion), channel_id=1, replica_groups=mesh['dp'=8,'mp'=4] {'dp'}, use_global_device_ids=true, to_apply=%region_11.12 | all-reduce | flops 128 | bytes 1024 | tf_op jit(solution)/shard_map/psum | solution.py:93
  (68 shorter events, 20.0 us)
Async XLA Ops:
  6.5 228.3 %reduce-scatter.3.cloned.1.call-start = ((), (), s32[]{:S(2)}) async-start(), calls=%async_computation.2 | async-start | bytes 2949120 | tf_op jit(solution)/shard_map/reduce_scatter | solution.py:69
  7.9 31.1 %collective-permute-start = (bf16[4,640,128]{1,2,0:T(8,128)(2,1)S(1)}, bf16[4,640,128]{1,2,0:T(8,128)(2,1)S(1)}, u32[]{:S(2)}, u32[]{:S(2)}) collective-permute-start(bf16[4,640,128]{1,2,0:T(8,128)(2,1)S(1)} %copy.8), channel_id=1, source_target_pairs={{0,4},{4,8},{8,12},{12,16},{16,20},{20,24},{24,28},{28,0},{1,5},{5... | collective-permute-start | bytes 1966088 | tf_op jit(solution)/shard_map/ppermute | solution.py:43
  11.0 40.0 %collective-permute-start.1 = (bf16[4,640,128]{1,2,0:T(8,128)(2,1)S(1)}, bf16[4,640,128]{1,2,0:T(8,128)(2,1)S(1)}, u32[]{:S(2)}, u32[]{:S(2)}) collective-permute-start(bf16[4,640,128]{1,2,0:T(8,128)(2,1)S(1)} %copy.8), channel_id=1, source_target_pairs={{0,28},{4,0},{8,4},{12,8},{16,12},{20,16},{24,20},{28,24},{1,29},{... | collective-permute-start | bytes 1966088 | tf_op jit(solution)/shard_map/ppermute | solution.py:50
  39.0 29.7 %collective-permute-start.2 = (bf16[4,640,128]{1,2,0:T(8,128)(2,1)S(1)}, bf16[4,640,128]{1,2,0:T(8,128)(2,1)S(1)}, u32[]{:S(2)}, u32[]{:S(2)}) collective-permute-start(bf16[4,640,128]{1,2,0:T(8,128)(2,1)S(1)} %collective-permute-done), channel_id=1, source_target_pairs={{0,4},{4,8},{8,12},{12,16},{16,20},{20,24},{24,28},{28,0},{1,5},{5... | collective-permute-start | bytes 1966088 | tf_op jit(solution)/shard_map/ppermute | solution.py:43
  51.0 35.6 %collective-permute-start.3 = (bf16[4,640,128]{1,2,0:T(8,128)(2,1)S(1)}, bf16[4,640,128]{1,2,0:T(8,128)(2,1)}, u32[]{:S(2)}, u32[]{:S(2)}) collective-permute-start(bf16[4,640,128]{1,2,0:T(8,128)(2,1)S(1)} %collective-permute-done.1), channel_id=1, source_target_pairs={{0,28},{4,0},{8,4},{12,8},{16,12},{20,16},{24,20},{28,24},{1,29},{... | collective-permute-start | bytes 1966088 | tf_op jit(solution)/shard_map/ppermute | solution.py:50
  68.7 30.9 %collective-permute-start.4 = (bf16[4,640,128]{1,2,0:T(8,128)(2,1)S(1)}, bf16[4,640,128]{1,2,0:T(8,128)(2,1)S(1)}, u32[]{:S(2)}, u32[]{:S(2)}) collective-permute-start(bf16[4,640,128]{1,2,0:T(8,128)(2,1)S(1)} %collective-permute-done.2), channel_id=1, source_target_pairs={{0,4},{4,8},{8,12},{12,16},{16,20},{20,24},{24,28},{28,0},{1,5},{5... | collective-permute-start | bytes 1966088 | tf_op jit(solution)/shard_map/ppermute | solution.py:43
  86.6 31.0 %collective-permute-start.5 = (bf16[4,640,128]{1,2,0:T(8,128)(2,1)}, bf16[4,640,128]{1,2,0:T(8,128)(2,1)}, u32[]{:S(2)}, u32[]{:S(2)}) collective-permute-start(bf16[4,640,128]{1,2,0:T(8,128)(2,1)} %collective-permute-done.3), channel_id=1, source_target_pairs={{0,28},{4,0},{8,4},{12,8},{16,12},{20,16},{24,20},{28,24},{1,29},{... | collective-permute-start | bytes 1966088 | tf_op jit(solution)/shard_map/ppermute | solution.py:50
  99.6 20.1 %collective-permute-start.6 = (bf16[4,640,128]{1,2,0:T(8,128)(2,1)S(1)}, bf16[4,640,128]{1,2,0:T(8,128)(2,1)S(1)}, u32[]{:S(2)}, u32[]{:S(2)}) collective-permute-start(bf16[4,640,128]{1,2,0:T(8,128)(2,1)S(1)} %collective-permute-done.4), channel_id=1, source_target_pairs={{0,4},{4,8},{8,12},{12,16},{16,20},{20,24},{24,28},{28,0},{1,5},{5... | collective-permute-start | bytes 1966088 | tf_op jit(solution)/shard_map/ppermute | solution.py:43
  120.6 17.0 %slice-start = ((s8[20971520]{0:T(1024)(128)(4,1)}), s8[4194304]{0:T(1024)(128)(4,1)S(1)}, s32[]{:S(2)}) async-start(s8[20971520]{0:T(1024)(128)(4,1)} %bitcast.64), calls=%async_computation.6 | async-start | bytes 8388608
  120.6 17.0 %slice-start.1 = ((s8[20971520]{0:T(1024)(128)(4,1)}), s8[4194304]{0:T(1024)(128)(4,1)S(1)}, s32[]{:S(2)}) async-start(s8[20971520]{0:T(1024)(128)(4,1)} %bitcast.64), calls=%async_computation.7 | async-start | bytes 8388608
  128.6 9.0 %slice-start.2 = ((s8[20971520]{0:T(1024)(128)(4,1)}), s8[4194304]{0:T(1024)(128)(4,1)S(1)}, s32[]{:S(2)}) async-start(s8[20971520]{0:T(1024)(128)(4,1)} %bitcast.64), calls=%async_computation.8 | async-start | bytes 8388608
  130.6 7.0 %slice-start.3 = ((s8[20971520]{0:T(1024)(128)(4,1)}), s8[4194304]{0:T(1024)(128)(4,1)S(1)}, s32[]{:S(2)}) async-start(s8[20971520]{0:T(1024)(128)(4,1)} %bitcast.64), calls=%async_computation.9 | async-start | bytes 8388608
  130.6 7.0 %slice-start.4 = ((s8[20971520]{0:T(1024)(128)(4,1)}), s8[4194304]{0:T(1024)(128)(4,1)S(1)}, s32[]{:S(2)}) async-start(s8[20971520]{0:T(1024)(128)(4,1)} %bitcast.64), calls=%async_computation.10 | async-start | bytes 8388608
  142.4 4.1 copy-start.3
  146.6 4.7 %copy-start.6 = (f32[512,384]{0,1:T(8,128)S(1)}, f32[512,384]{0,1:T(8,128)}, u32[]{:S(2)}) copy-start(f32[512,384]{0,1:T(8,128)} %fusion.30) | copy-start | bytes 2359300
  146.6 4.7 %copy-start.7 = (f32[512,384]{0,1:T(8,128)S(1)}, f32[512,384]{0,1:T(8,128)}, u32[]{:S(2)}) copy-start(f32[512,384]{0,1:T(8,128)} %fusion.33) | copy-start | bytes 2359300
  151.2 1.1 copy-start.8
  152.7 7.6 %copy-start.9 = (f32[1,5120]{1,0:T(1,128)S(1)}, f32[1,5120]{1,0:T(1,128)}, u32[]{:S(2)}) copy-start(f32[1,5120]{1,0:T(1,128)} %get-tuple-element.24) | copy-start | bytes 61444
  166.3 112.5 %all-gather.3.cloned.1.call-start = ((), (), s32[]{:S(2)}) async-start(), calls=%async_computation.3 | async-start | bytes 1474560 | tf_op jit(solution)/shard_map/all_gather | solution.py:72
  236.5 135.6 %reduce-scatter.5.cloned.1.call-start = ((), (), s32[]{:S(2)}) async-start(), calls=%async_computation.4 | async-start | bytes 2949120 | tf_op jit(solution)/shard_map/reduce_scatter | solution.py:77
  290.4 10.0 %copy-start = (bf16[5120,128]{0,1:T(8,128)(2,1)S(1)}, bf16[5120,128]{0,1:T(8,128)(2,1)}, u32[]{:S(2)}) copy-start(bf16[5120,128]{0,1:T(8,128)(2,1)} %all-gather.3.cloned.1.call-done) | copy-start | bytes 3932164
  302.4 71.5 %copy-start.2 = (bf16[4,640,128]{2,1,0:T(8,128)(2,1)S(1)}, bf16[4,640,128]{2,1,0:T(8,128)(2,1)}, u32[]{:S(2)}) copy-start(bf16[4,640,128]{2,1,0:T(8,128)(2,1)} %param.3) | copy-start | bytes 1966084
  302.4 113.6 %all-gather.5.cloned.1.call-start = ((), (), s32[]{:S(2)}) async-start(), calls=%async_computation.5 | async-start | bytes 1474560 | tf_op jit(solution)/shard_map/all_gather | solution.py:83
  416.0 2.0 copy-start.1
  419.8 30.2 %copy-start.4 = (f32[640,128]{0,1:T(8,128)S(1)}, f32[640,128]{0,1:T(8,128)}, u32[]{:S(2)}) copy-start(f32[640,128]{0,1:T(8,128)} %reduce-scatter.3.cloned.1.call-done) | copy-start | bytes 983044
  419.8 30.1 %copy-start.5 = (f32[640,128]{0,1:T(8,128)S(1)}, f32[640,128]{0,1:T(8,128)}, u32[]{:S(2)}) copy-start(f32[640,128]{0,1:T(8,128)} %reduce-scatter.5.cloned.1.call-done) | copy-start | bytes 983044
Sparse Core Ops, SparseCore 0:
  166.5 68.3 reduce-scatter.2
  237.1 41.6 all-gather.2
  302.5 69.5 reduce-scatter.4
  374.3 41.6 all-gather.4
